TPU v7x, 512 devices: a whole 4x8x8 slice. The times are simulated.
512 devices in a mesh: aux: 32 (over y, x), ao: 16 (over z, core).
Axes of the slice: x: 4, y: 8, z: 8, core: 2. Of those that a mesh axis runs over, the one named last changes fastest.
Arguments:
- tile_values: bfloat16 [8192, 48, 2304], P(('aux', 'ao')), may hold values from -6 to 6
- tile_owner: int32 [8192, 1], P(('aux', 'ao')), may hold values from 0 to 15; in each aligned block of 16 rows (0 to 15, 16 to 31, ...) at most 2 rows name the same one
- tile_block: int32 [8192], P(('aux', 'ao')), may hold values from 0 to 7
- coefficients: bfloat16 [128, 48, 512], P('ao'), may hold values from -0.21875 to 0.21875
Outputs:
- exchange_band: float32 [16, 3840], P('ao', 'aux')
Inputs may be any that keep to these rules, and one draw needn't show every extreme that they name: `tile_owner`: among the 16 tiles of one device at most 2 name the same ao index, and in some device exactly 2 do.
All inputs are finite; a program needn't handle non-finite values.
Results may differ from a plain program's by a relative error of at most 0.004.
Values may be sent and summed in bfloat16 or wider, within the bound.
A program may use at most 64 MiB of HBM per device.

v0:
```python
import math

import jax
import jax.numpy as jnp
from jax import lax
from jax.sharding import PartitionSpec as P

HW = 16


def extended_2(cells, sides, width):
    for axis, dim in sides:
        count = lax.axis_size(axis)
        ends = count - 1
        head = lax.slice_in_dim(cells, 0, width, axis=dim)
        tail = lax.slice_in_dim(cells, cells.shape[dim] - width, cells.shape[dim], axis=dim)
        cells = jnp.concatenate(
            [
                lax.ppermute(tail, axis, [(i, (i + 1) % count) for i in range(ends)]),
                cells,
                lax.ppermute(head, axis, [((i + 1) % count, i) for i in range(ends)]),
            ],
            axis=dim,
        )
    return cells


def same_owner_rank(owners):
    count = owners.shape[-1]
    equal = owners[..., :, None] == owners[..., None, :]
    earlier = jnp.arange(count)[None, :] < jnp.arange(count)[:, None]
    return jnp.sum(jnp.logical_and(equal, earlier), axis=-1)


def ragged_rows(tile_owner, tile_block, coefficients):
    tile_count = tile_block.shape[0]
    groups = lax.axis_size("ao")
    capacity = max(2, -(-tile_count // groups))
    held = coefficients.shape[0]
    my_index = lax.axis_index("ao")
    all_owners, all_blocks = (
        lax.all_gather(tile_owner, "ao", axis=0, tiled=True),
        lax.all_gather(tile_block, "ao", axis=0, tiled=True),
    )
    peer_owners = all_owners[:, 0].reshape(groups, tile_count)
    peer_blocks = all_blocks.reshape(groups, tile_count)
    peer_rank = same_owner_rank(peer_owners)
    slot_range = jnp.arange(capacity, dtype=jnp.int32)
    block_range = jnp.arange(held, dtype=jnp.int32)
    outgoing = jnp.logical_and(
        (peer_owners == my_index)[:, :, None], peer_rank[:, :, None] == slot_range
    )
    which_block = peer_blocks[:, :, None] == block_range
    selection = jnp.einsum(
        "dtc,dtb->dcb", outgoing.astype(jnp.float32), which_block.astype(jnp.float32)
    ).astype(jnp.bfloat16)
    send_buffer = jnp.einsum(
        "dcb,blk->dclk", selection, coefficients, preferred_element_type=jnp.float32
    ).astype(jnp.bfloat16)
    received = lax.all_to_all(send_buffer, "ao", split_axis=0, concat_axis=0, tiled=True)
    owners = tile_owner[:, 0]
    my_rank = same_owner_rank(owners)
    owner_range = jnp.arange(groups, dtype=jnp.int32)
    pick_table = jnp.logical_and(
        (owners[:, None] == owner_range)[:, :, None], (my_rank[:, None] == slot_range)[:, None, :]
    )
    return jnp.einsum(
        "toc,oclk->tlk",
        pick_table.astype(jnp.bfloat16),
        received,
        preferred_element_type=jnp.float32,
    ).astype(jnp.bfloat16)


def transform(tile_rows, tile_grid):
    return jnp.einsum(
        "tlc,tlmp->mcp", tile_rows, tile_grid, preferred_element_type=jnp.float32
    ).astype(jnp.bfloat16)


def extend(response):
    return extended_2(response, (("ao", 0),), HW)


def local(tile_values, tile_owner, tile_block, coefficients):
    tile_count = tile_values.shape[0]
    block_size = tile_values.shape[1]
    columns = coefficients.shape[2]
    occupied = columns // 2
    tile_rows = ragged_rows(tile_owner, tile_block, coefficients)
    tile_grid = tile_values.reshape(tile_count, block_size, block_size, block_size)
    both_sides = transform(tile_rows, tile_grid)
    occupied_side = both_sides[:, :occupied, :].reshape(block_size, occupied * block_size)
    response = both_sides[:, occupied:, :].reshape(block_size, occupied * block_size)
    extended = extend(response)
    band_block = lax.dot_general(
        occupied_side, extended, (((1,), (1,)), ((), ())), preferred_element_type=jnp.float32
    )
    flattened = band_block.reshape(1, -1)
    factor = 1.0 / math.sqrt(occupied * block_size * lax.axis_size("aux"))
    return lax.psum_scatter(flattened, "aux", scatter_dimension=1, tiled=True) * factor


def solution(mesh):
    placed = (
        P(("aux", "ao"), None, None),
        P(("aux", "ao"), None),
        P(("aux", "ao")),
        P("ao", None, None),
    )
    return jax.shard_map(
        local, mesh=mesh, in_specs=placed, out_specs=P("ao", "aux"), check_vma=False
    )
```

profile of v0, /device:TPU:64, one launch (start us, length us, event | category | flops | bytes accessed | tf_op | source)
XLA Modules:
  0.0 264.2 jit_solution(13833545462061784308)
XLA Ops:
  0.0 1.3 dynamic-slice
  1.9 0.8 bitcast_dynamic-update-slice_fusion
  2.7 0.8 dynamic-update-slice.1
  3.5 18.0 %all-reduce.3 = (s32[256]{0:T(256)S(1)}, s32[256]{0:T(256)S(1)}) all-reduce(s32[256]{0:T(256)S(1)} %dynamic-update-slice.1, s32[256]{0:T(256)S(1)} %bitcast_dynamic-update-slice_fusion), channel_id=1, replica_groups=mesh['aux'=32,'ao'=16] {'ao'}, use_global_device_ids=true, to_apply=%add.1 | all-reduce | flops 512 | bytes 4096
  21.5 0.1 reshape_squeeze.3
  21.6 0.4 convert_reduce_fusion
  22.0 0.1 eq.117
  22.1 0.2 fusion.18
  22.3 1.6 convolution_convert_fusion
  23.8 0.0 copy-start
  23.8 2.0 copy.31
  25.8 5.3 %all-to-all-start = ((bf16[16,2,48,512]{3,2,1,0:T(8,128)(2,1)}), bf16[16,2,48,512]{3,2,1,0:T(8,128)(2,1)}, u32[]{:S(2)}, u32[]{:S(2)}) async-start(bf16[16,2,48,512]{3,2,1,0:T(8,128)(2,1)} %copy.31), calls=%async_computation | async-start | bytes 3145728 | tf_op jit(solution)/shard_map/all_to_all | solution.py:60
  31.1 0.0 copy-done
  31.1 0.0 copy-start.1
  31.1 14.0 %reshape.75 = bf16[16,48,48,48]{3,2,1,0:T(8,128)(2,1)} reshape(bf16[16,48,2304]{2,1,0:T(8,128)(2,1)S(1)} %copy-done) | data formatting | bytes 7077888 | tf_op jit(solution)/shard_map/reshape | solution.py:91
  45.2 0.0 copy-done.1
  45.2 0.2 convert_reduce_fusion.1
  45.4 0.1 iota_compare_fusion.3
  45.4 21.8 %all-to-all-done = bf16[16,2,48,512]{3,2,1,0:T(8,128)(2,1)} async-done(((bf16[16,2,48,512]{3,2,1,0:T(8,128)(2,1)}), bf16[16,2,48,512]{3,2,1,0:T(8,128)(2,1)}, u32[]{:S(2)}, u32[]{:S(2)}) %all-to-all-start) | async-done | bytes 1572896 | tf_op jit(solution)/shard_map/all_to_all | solution.py:60
  67.3 11.3 %fusion.2 = bf16[48,512,48]{1,2,0:T(8,128)(2,1)S(1)} fusion(bf16[16,48,48,48]{3,2,1,0:T(8,128)(2,1)} %reshape.75, bf16[16,2,48,512]{3,2,1,0:T(8,128)(2,1)} %all-to-all-done, pred[16,2]{0,1:T(4,128)(4,1)S(1)} %iota_compare_fusion.4, pred[16,16]{1,0:T(8,128)(4,1)S(1)} %iota_compare_fusion.3), kind=kOutput, calls=%fused_computation.3 | convolution fusion | flops 1838678528 | bytes 7471392 | tf_op jit(solution)/shard_map/tlc,tlmp->mcp/dot_general | solution.py:76
  78.6 0.9 fusion.31
  79.5 1.5 copy.35
  81.0 2.8 %slice.22 = bf16[16,12288]{1,0:T(8,128)(2,1)} reshape(bf16[16,256,48]{2,1,0:T(8,128)(2,1)S(1)} %copy.35) | data formatting | bytes 786432 | tf_op jit(solution)/shard_map/slice | solution.py:16
  83.8 2.4 collective-permute-start
  86.2 1.5 copy.37
  87.7 2.8 %slice.25 = bf16[16,12288]{1,0:T(8,128)(2,1)} reshape(bf16[16,256,48]{2,1,0:T(8,128)(2,1)S(1)} %copy.37) | data formatting | bytes 786432 | tf_op jit(solution)/shard_map/slice | solution.py:15
  90.5 4.2 %collective-permute-start.1 = (bf16[16,12288]{1,0:T(8,128)(2,1)}, bf16[16,12288]{1,0:T(8,128)(2,1)S(1)}, u32[]{:S(2)}, u32[]{:S(2)}) collective-permute-start(bf16[16,12288]{1,0:T(8,128)(2,1)} %slice.25), channel_id=1, source_target_pairs={{1,0},{2,1},{3,2},{4,3},{5,4},{6,5},{7,6},{8,7},{9,8},{10,9},{11,1... | collective-permute-start | bytes 1179656 | tf_op jit(solution)/shard_map/ppermute | solution.py:21
  94.6 1.3 dynamic-slice.2
  96.6 1.6 fusion.32
  98.2 3.0 %copy.34 = bf16[48,256,48]{2,1,0:T(8,128)(2,1)S(1)} copy(bf16[48,256,48]{1,2,0:T(8,128)(2,1)} %get-tuple-element.10) | data formatting | bytes 2359296 | tf_op jit(solution)/shard_map/slice | solution.py:93
  101.1 6.9 %reshape.76 = bf16[48,12288]{1,0:T(8,128)(2,1)} reshape(bf16[48,256,48]{2,1,0:T(8,128)(2,1)S(1)} %copy.34) | data formatting | bytes 2359296 | tf_op jit(solution)/shard_map/reshape | solution.py:93
  108.0 3.0 %copy.36 = bf16[48,256,48]{2,1,0:T(8,128)(2,1)S(1)} copy(bf16[48,256,48]{1,2,0:T(8,128)(2,1)} %get-tuple-element.9) | data formatting | bytes 2359296 | tf_op jit(solution)/shard_map/slice | solution.py:94
  111.0 6.9 %reshape.77 = bf16[48,12288]{1,0:T(8,128)(2,1)} reshape(bf16[48,256,48]{2,1,0:T(8,128)(2,1)S(1)} %copy.36) | data formatting | bytes 2359296 | tf_op jit(solution)/shard_map/reshape | solution.py:94
  117.8 0.0 collective-permute-done
  117.9 0.0 collective-permute-done.1
  117.9 2.4 fusion.5
  120.2 0.1 reshape.78
  120.3 143.3 %all-reduce.2 = f32[1,3840]{1,0:T(1,128)S(1)} all-reduce(f32[1,3840]{1,0:T(1,128)S(1)} %reshape.78), channel_id=2, replica_groups=mesh['aux'=32,'ao'=16] {'aux'}, use_global_device_ids=true, to_apply=%region_2.0.clone | all-reduce | flops 3840 | bytes 30720
  263.7 0.6 dynamic-slice_multiply_fusion
  (5 shorter events, 0.0 us)
Async XLA Ops:
  23.8 7.3 %copy-start = (bf16[16,48,2304]{2,1,0:T(8,128)(2,1)S(1)}, bf16[16,48,2304]{2,1,0:T(8,128)(2,1)}, u32[]{:S(2)}) copy-start(bf16[16,48,2304]{2,1,0:T(8,128)(2,1)} %param.4) | copy-start | bytes 10616836
  25.8 41.4 %all-to-all-start = ((bf16[16,2,48,512]{3,2,1,0:T(8,128)(2,1)}), bf16[16,2,48,512]{3,2,1,0:T(8,128)(2,1)}, u32[]{:S(2)}, u32[]{:S(2)}) async-start(bf16[16,2,48,512]{3,2,1,0:T(8,128)(2,1)} %copy.31), calls=%async_computation | async-start | bytes 3145728 | tf_op jit(solution)/shard_map/all_to_all | solution.py:60
  31.1 14.0 %copy-start.1 = (s32[16,1]{0,1:T(1,128)S(1)}, s32[16,1]{0,1:T(1,128)}, u32[]{:S(2)}) copy-start(s32[16,1]{0,1:T(1,128)} %param.5) | copy-start | bytes 196
  83.8 34.0 %collective-permute-start = (bf16[16,12288]{1,0:T(8,128)(2,1)}, bf16[16,12288]{1,0:T(8,128)(2,1)}, u32[]{:S(2)}, u32[]{:S(2)}) collective-permute-start(bf16[16,12288]{1,0:T(8,128)(2,1)} %slice.22), channel_id=1, source_target_pairs={{0,1},{1,2},{2,3},{3,4},{4,5},{5,6},{6,7},{7,8},{8,9},{9,10},{10,1... | collective-permute-start | bytes 1179656 | tf_op jit(solution)/shard_map/ppermute | solution.py:19
  90.5 27.4 %collective-permute-start.1 = (bf16[16,12288]{1,0:T(8,128)(2,1)}, bf16[16,12288]{1,0:T(8,128)(2,1)S(1)}, u32[]{:S(2)}, u32[]{:S(2)}) collective-permute-start(bf16[16,12288]{1,0:T(8,128)(2,1)} %slice.25), channel_id=1, source_target_pairs={{1,0},{2,1},{3,2},{4,3},{5,4},{6,5},{7,6},{8,7},{9,8},{10,9},{11,1... | collective-permute-start | bytes 1179656 | tf_op jit(solution)/shard_map/ppermute | solution.py:21
where the time goes:
time: 265 us; the launch traced here: 264 us
  blocking collectives  161 us (61%)
  local copies, waits for them, and re-layouts  51.1 us (19%)
  waiting for transfers between devices  21.8 us (8%)
  matrix products  15.4 us (6%)
  starting transfers between devices  11.9 us (4%)
    unnamed x2, blocking collectives  161 us
    all_to_all x1, waiting for transfers between devices, ragged_rows(): lax.all_to_all(send_buffer, 'ao', split_axis=0, concat_axis=0, tiled=True)  21.8 us
    reshape x1, local copies, waits for them, and re-layouts, local(): tile_values.reshape(tile_count, block_size, block_size, block_size)  14 us
    dot_general x1, matrix products, transform(): jnp.einsum('tlc,tlmp->mcp', tile_rows, tile_grid, preferred_element_type=...  11.3 us
    reshape x1, local copies, waits for them, and re-layouts, local(): both_sides[:, occupied:, :].reshape(block_size, occupied * block_size)  6.88 us
    reshape x1, local copies, waits for them, and re-layouts, local(): both_sides[:, :occupied, :].reshape(block_size, occupied * block_size)  6.85 us
  transfers between devices with their start and end apart: 3, of which 1 were waited for; matrix products, arithmetic and copies ran while one was open for 16% of the time, Pallas kernels for 0%

commit v1 on v0

v1 whole, which is shorter than its diff:
```python
import functools
import math

import jax
import jax.numpy as jnp
from jax import lax
from jax.experimental import pallas as pl
from jax.experimental.pallas import tpu as pltpu
from jax.sharding import PartitionSpec as P

X = 4
BS = 48
HW = 16
PB = 16
NN = (((1,), (0,)), ((), ()))
NT = (((1,), (1,)), ((), ()))


def dot(a, b, dims):
    return lax.dot_general(a, b, dims, preferred_element_type=jnp.float32)


def kernel(
    Y, Z, factor,
    owner_ref, block_ref, tiles_ref, coef_ref, out_ref,
    tiles, perm, tt, cg, picked, occ, rsp, halo, band, send1, recv1, send2, recv2, idx_v, idx_s,
    tile_sem, coef_sem, sis_send, sis_recv, ring_send, ring_recv, tt_send, tt_recv,
    idx_send, idx_recv, idx_sem, halo_send, halo_recv, s1_send, s1_recv, s2_send, s2_recv,
):
    aux, ao = lax.axis_index("aux"), lax.axis_index("ao")
    y, x = aux // X, aux % X
    z, core = ao // 2, ao % 2
    other = 1 - core
    held = coef_ref.shape[0]
    per = 2 * held
    half = Z // 2
    group = 2 * X
    spot = x * 2 + core

    def at_z(step):
        return {"aux": aux, "ao": lax.rem(z + step + Z, Z) * 2 + core}

    def at_group(step):
        there = lax.rem(spot + step, group)
        return {"aux": y * X + there // 2, "ao": z * 2 + there % 2}

    def at_y(step):
        return {"aux": lax.rem(y + step, Y) * X + x, "ao": ao}

    sister = {"aux": aux, "ao": z * 2 + other}

    def remote(src, dst, send, recv, where):
        return pltpu.make_async_remote_copy(
            src_ref=src, dst_ref=dst, send_sem=send, recv_sem=recv,
            device_id=where, device_id_type=pl.DeviceIdType.MESH,
        )

    tile_copy = pltpu.make_async_copy(tiles_ref, tiles, tile_sem)
    tile_copy.start()

    barrier = pltpu.get_barrier_semaphore()
    peers = [at_z(1), at_z(-1)] + [at_group(d) for d in range(1, group)] + [at_y(d) for d in range(1, Y)]
    for peer in peers:
        pl.semaphore_signal(barrier, inc=1, device_id=peer, device_id_type=pl.DeviceIdType.MESH)

    mine = ao * held
    local, swap = [], []
    for part in range(2):
        own = pl.ds(pl.multiple_of(part * 256 + core * 128, 128), 128)
        theirs = pl.ds(pl.multiple_of(part * 256 + other * 128, 128), 128)
        into = cg.at[pl.ds(mine, held), :, pl.ds(part * 128, 128)]
        local.append(pltpu.make_async_copy(coef_ref.at[:, :, own], into, coef_sem.at[part]))
        swap.append(remote(coef_ref.at[:, :, theirs], into, sis_send.at[part], sis_recv.at[part], sister))
    for copy in local:
        copy.start()

    lane = lax.broadcasted_iota(jnp.int32, (8, 128), 1)
    listed = jnp.zeros((8, 128), jnp.int32)
    for t in range(16):
        listed = jnp.where(lane == t, owner_ref[t] * held + block_ref[t], listed)
    idx_v[0] = listed

    pl.semaphore_wait(barrier, len(peers))
    for copy in swap:
        copy.start()
    idx_copy = remote(idx_v.at[0], idx_v.at[1], idx_send, idx_recv, sister)
    idx_copy.start()

    rows = lax.broadcasted_iota(jnp.int32, (768, 768), 0)
    want = (rows & 15) * BS + (rows >> 4)
    perm[...] = (lax.broadcasted_iota(jnp.int32, (768, 768), 1) == want).astype(jnp.bfloat16)

    for copy in local:
        copy.wait()
    for copy in swap:
        copy.wait()

    def ring(step):
        ups, downs = lax.rem(z - (step - 1) + Z, Z), lax.rem(z + (step - 1), Z)
        size = held if step == half else per
        up = cg.at[pl.ds(ups * per, size)]
        down = cg.at[pl.ds(downs * per + (per - size), size)]
        return [
            remote(up, up, ring_send.at[0, step - 1], ring_recv.at[0, step - 1], at_z(1)),
            remote(down, down, ring_send.at[1, step - 1], ring_recv.at[1, step - 1], at_z(-1)),
        ]

    def turn(part):
        rhs = tiles[:, :, part * 768:(part + 1) * 768].reshape(768, 768)

        def body(i, carry):
            start = pl.multiple_of(i * 256, 256)
            got = dot(perm[pl.ds(start, 256), :], rhs, NT).astype(jnp.bfloat16)
            tt[core, pl.ds(i * 16, 16), part * 16:(part + 1) * 16, :] = got.reshape(16, 16, 768)
            return carry

        lax.fori_loop(0, 3, body, 0)

    tt_copy = remote(tt.at[core], tt.at[core], tt_send, tt_recv, sister)
    for step in range(1, half + 1):
        copies = ring(step)
        for copy in copies:
            copy.start()
        if step == 1:
            tile_copy.wait()
            for part in range(3):
                turn(part)
            tt_copy.start()
        if step == 2:
            idx_copy.wait()
            fetch = pltpu.make_async_copy(idx_v.at[1], idx_s, idx_sem)
            fetch.start()
            fetch.wait()
        for copy in copies:
            copy.wait()
    tt_copy.wait()

    for t in range(16):
        picked[core, t * BS:(t + 1) * BS, :] = cg[owner_ref[t] * held + block_ref[t]]
        picked[other, t * BS:(t + 1) * BS, :] = cg[idx_s[0, t]]

    halos = []
    for b in range(BS // PB):
        ps = pl.ds(b * PB, PB)
        for r in range(2):
            right = picked[r]

            def body(i, carry):
                p = b * PB + i * 8
                got = dot(tt[r, pl.ds(p, 8)].reshape(8 * BS, 768), right, NN).astype(jnp.bfloat16)
                got = got.reshape(8, BS, 256)
                occ[pl.ds(p, 8), r * BS:(r + 1) * BS, :] = got[:, :, :128]
                rsp[pl.ds(p, 8), r * BS:(r + 1) * BS, :] = got[:, :, 128:]
                return carry

            lax.fori_loop(0, PB // 8, body, 0)
        down = remote(rsp.at[ps, 0:HW], halo.at[1, ps], halo_send.at[1, b], halo_recv.at[1, b], at_z(-1))
        up = remote(rsp.at[ps, 2 * BS - HW:2 * BS], halo.at[0, ps], halo_send.at[0, b], halo_recv.at[0, b], at_z(1))
        down.start()
        up.start()
        halos += [(down, up)]

    total = jnp.zeros((2 * BS, 2 * BS + 2 * HW), jnp.float32)
    for b in range(BS // PB):
        for copy in halos[b]:
            copy.wait()
        left, wide = [], []
        for p in range(b * PB, (b + 1) * PB):
            left.append(occ[p])
            wide.append(jnp.concatenate([halo[0, p], rsp[p], halo[1, p]], axis=0))
        total = total + dot(jnp.concatenate(left, axis=1), jnp.concatenate(wide, axis=1), NT)

    shape = (2 * BS, 2 * BS + 2 * HW)
    at_row, at_col = lax.broadcasted_iota(jnp.int32, shape, 0), lax.broadcasted_iota(jnp.int32, shape, 1)
    outside = jnp.logical_or(
        jnp.logical_and(z == 0, at_col < HW), jnp.logical_and(z == Z - 1, at_col >= 2 * BS + HW)
    )
    band[...] = jnp.where(outside, 0.0, total)

    for there in range(group):
        xx, c = there // 2, there % 2
        first = c * BS + 3 * (xx // 2)
        shift = BS * c
        if xx % 2 == 0:
            one, two = band[pl.ds(first, 8, stride=6), :], band[pl.ds(first + 1, 8, stride=6), :]
            a, b, cut = (128 - shift) % 128, (80 - shift) % 128, 80
        else:
            one, two = band[pl.ds(first + 1, 8, stride=6), :], band[pl.ds(first + 2, 8, stride=6), :]
            a, b, cut = (128 - shift - 40) % 128, (40 - shift) % 128, 40
        one = pltpu.roll(one, a, 1) if a else one
        two = pltpu.roll(two, b, 1) if b else two
        send1[there] = jnp.where(lane < cut, one, two)

    copies = []
    for d in range(1, group):
        there = lax.rem(spot + d, group)
        copies.append(remote(send1.at[there], recv1.at[d], s1_send.at[d], s1_recv.at[d], at_group(d)))
        copies[-1].start()
    partial = send1[spot]
    for d in range(1, group):
        copies[d - 1].wait()
        partial = partial + recv1[d]
    send2[...] = partial
    copies = []
    for d in range(1, Y):
        copies.append(remote(send2, recv2.at[d], s2_send.at[d], s2_recv.at[d], at_y(d)))
        copies[-1].start()
    for d in range(1, Y):
        copies[d - 1].wait()
        partial = partial + recv2[d]
    row = lax.broadcasted_iota(jnp.int32, (8, 128), 0)
    out_ref[...] = jnp.sum(jnp.where(row == y, partial, 0.0), axis=0, keepdims=True) * factor


def local(tile_values, tile_owner, tile_block, coefficients):
    n_aux, n_ao = lax.axis_size("aux"), lax.axis_size("ao")
    Y, Z = n_aux // X, n_ao // 2
    count = tile_values.shape[0]
    held = coefficients.shape[0]
    factor = 1.0 / math.sqrt(256 * BS * n_aux)
    bf, f32 = jnp.bfloat16, jnp.float32
    dma = pltpu.SemaphoreType.DMA
    got = pl.pallas_call(
        functools.partial(kernel, Y, Z, factor),
        out_shape=jax.ShapeDtypeStruct((1, 128), f32),
        in_specs=[
            pl.BlockSpec(memory_space=pltpu.SMEM),
            pl.BlockSpec(memory_space=pltpu.SMEM),
            pl.BlockSpec(memory_space=pl.ANY),
            pl.BlockSpec(memory_space=pl.ANY),
        ],
        out_specs=pl.BlockSpec(memory_space=pltpu.VMEM),
        scratch_shapes=[
            pltpu.VMEM((count, BS, BS * BS), bf),
            pltpu.VMEM((768, 768), bf),
            pltpu.VMEM((2, BS, BS, 768), bf),
            pltpu.VMEM((n_ao * held, BS, 256), bf),
            pltpu.VMEM((2, 768, 256), bf),
            pltpu.VMEM((BS, 2 * BS, 128), bf),
            pltpu.VMEM((BS, 2 * BS, 128), bf),
            pltpu.VMEM((2, BS, HW, 128), bf),
            pltpu.VMEM((2 * BS, 2 * BS + 2 * HW), f32),
            pltpu.VMEM((2 * X, 8, 128), f32),
            pltpu.VMEM((2 * X, 8, 128), f32),
            pltpu.VMEM((8, 128), f32),
            pltpu.VMEM((Y, 8, 128), f32),
            pltpu.VMEM((2, 8, 128), jnp.int32),
            pltpu.SMEM((8, 128), jnp.int32),
            dma, dma((2,)), dma((2,)), dma((2,)),
            dma((2, Z // 2)), dma((2, Z // 2)), dma, dma,
            dma, dma, dma,
            dma((2, BS // PB)), dma((2, BS // PB)),
            dma((2 * X,)), dma((2 * X,)), dma((Y,)), dma((Y,)),
        ],
        compiler_params=pltpu.CompilerParams(
            collective_id=0, has_side_effects=True, vmem_limit_bytes=48 * 1024 * 1024
        ),
        name="exchange",
    )(tile_owner.reshape(count), tile_block, tile_values, coefficients)
    return got[:, :BS * (BS + 2 * HW) // n_aux]


def solution(mesh):
    placed = (
        P(("aux", "ao"), None, None),
        P(("aux", "ao"), None),
        P(("aux", "ao")),
        P("ao", None, None),
    )
    return jax.shard_map(
        local, mesh=mesh, in_specs=placed, out_specs=P("ao", "aux"), check_vma=False
    )
```

time: 265 us -> 75.4 us (0.28)
  the two profiles are of different devices: /device:TPU:64 before, /device:TPU:1 now
where the time goes in v1:
time: 75.4 us; the launch traced here: 75.2 us
  Pallas kernels  70.4 us (93%)
  local copies, waits for them, and re-layouts  4.82 us (6%)
    pallas_call x1, Pallas kernels, local(): pl.pallas_call(functools.partial(kernel, Y, Z, factor), out_shape=jax.Sha...  70.4 us
    unnamed x9, local copies, waits for them, and re-layouts  4.82 us

profile of v1, /device:TPU:1, one launch (start us, length us, event | category | flops | bytes accessed | tf_op | source)
XLA Modules:
  0.0 75.2 jit_solution(8461237235776576634)
XLA Ops:
  0.0 0.0 copy-start
  0.0 2.0 %copy-done = bf16[16,48,2304]{2,1,0:T(8,128)(2,1)S(1)} copy-done((bf16[16,48,2304]{2,1,0:T(8,128)(2,1)S(1)}, bf16[16,48,2304]{2,1,0:T(8,128)(2,1)}, u32[]{:S(2)}) %copy-start) | copy-done | bytes 3538968
  2.0 0.0 copy-start.1
  2.0 1.0 %copy-done.1 = bf16[8,48,512]{2,1,0:T(8,128)(2,1)S(1)} copy-done((bf16[8,48,512]{2,1,0:T(8,128)(2,1)S(1)}, bf16[8,48,512]{2,1,0:T(8,128)(2,1)}, u32[]{:S(2)}) %copy-start.1) | copy-done | bytes 393240
  3.0 0.0 copy-start.2
  3.0 0.7 copy-done.2
  3.7 0.0 copy-start.3
  3.7 0.7 copy-done.3
  4.3 70.4 %exchange.1 = f32[1,128]{1,0:T(1,128)S(1)} custom-call(s32[16]{0:T(128)S(1)} %bitcast.2, s32[16]{0:T(128)S(1)} %copy-done.3, bf16[16,48,2304]{2,1,0:T(8,128)(2,1)S(1)} %copy-done, bf16[8,48,512]{2,1,0:T(8,128)(2,1)S(1)} %copy-done.1), custom_call_target="tpu_custom_call" | custom-call | tf_op jit(solution)/shard_map/exchange/pallas_call | solution.py:223
  74.7 0.5 copy.6
Async XLA Ops:
  0.0 2.0 %copy-start = (bf16[16,48,2304]{2,1,0:T(8,128)(2,1)S(1)}, bf16[16,48,2304]{2,1,0:T(8,128)(2,1)}, u32[]{:S(2)}) copy-start(bf16[16,48,2304]{2,1,0:T(8,128)(2,1)} %tiles_ref.1) | copy-start | bytes 10616836
  2.0 1.0 %copy-start.1 = (bf16[8,48,512]{2,1,0:T(8,128)(2,1)S(1)}, bf16[8,48,512]{2,1,0:T(8,128)(2,1)}, u32[]{:S(2)}) copy-start(bf16[8,48,512]{2,1,0:T(8,128)(2,1)} %coef_ref.1) | copy-start | bytes 1179652
  3.0 0.7 copy-start.2
  3.7 0.7 copy-start.3

commit v2 on v1

--- a/solution.py
+++ b/solution.py
@@ -11,7 +11,8 @@
 X = 4
 BS = 48
 HW = 16
-PB = 16
+PB = 8
+SUBS = 4
 NN = (((1,), (0,)), ((), ()))
 NT = (((1,), (1,)), ((), ()))
 
@@ -22,9 +23,10 @@
 
 def kernel(
     Y, Z, factor,
-    owner_ref, block_ref, tiles_ref, coef_ref, out_ref,
+    owner_hbm, block_hbm, tiles_ref, coef_ref, out_ref,
+    owner_ref, block_ref,
     tiles, perm, tt, cg, picked, occ, rsp, halo, band, send1, recv1, send2, recv2, idx_v, idx_s,
-    tile_sem, coef_sem, sis_send, sis_recv, ring_send, ring_recv, tt_send, tt_recv,
+    list_sem, tile_sem, coef_sem, sis_send, sis_recv, ring_send, ring_recv, tt_send, tt_recv,
     idx_send, idx_recv, idx_sem, halo_send, halo_recv, s1_send, s1_recv, s2_send, s2_recv,
 ):
     aux, ao = lax.axis_index("aux"), lax.axis_index("ao")
@@ -57,6 +59,12 @@
 
     tile_copy = pltpu.make_async_copy(tiles_ref, tiles, tile_sem)
     tile_copy.start()
+    lists = [
+        pltpu.make_async_copy(owner_hbm, owner_ref, list_sem.at[0]),
+        pltpu.make_async_copy(block_hbm, block_ref, list_sem.at[1]),
+    ]
+    for copy in lists:
+        copy.start()
 
     barrier = pltpu.get_barrier_semaphore()
     peers = [at_z(1), at_z(-1)] + [at_group(d) for d in range(1, group)] + [at_y(d) for d in range(1, Y)]
@@ -74,36 +82,48 @@
     for copy in local:
         copy.start()
 
+    rows = lax.broadcasted_iota(jnp.int32, (768, 768), 0)
+    want = (rows & 15) * BS + (rows >> 4)
+    perm[...] = (lax.broadcasted_iota(jnp.int32, (768, 768), 1) == want).astype(jnp.bfloat16)
+
+    pl.semaphore_wait(barrier, len(peers))
+    for copy in swap:
+        copy.start()
+
+    size = per // SUBS
+
+    def hop(step, sub):
+        spot_in = lax.rem(sub + core * (SUBS // 2), SUBS) * size
+        ups, downs = lax.rem(z - (step - 1) + Z, Z), lax.rem(z + (step - 1), Z)
+        up, down = cg.at[pl.ds(ups * per + spot_in, size)], cg.at[pl.ds(downs * per + spot_in, size)]
+        copies = []
+        if step < half or sub % 2 == 0:
+            copies.append(remote(up, up, ring_send.at[0, step - 1, sub], ring_recv.at[0, step - 1, sub], at_z(1)))
+        if step < half or sub % 2 == 1:
+            copies.append(remote(down, down, ring_send.at[1, step - 1, sub], ring_recv.at[1, step - 1, sub], at_z(-1)))
+        for copy in copies:
+            copy.start()
+        return copies
+
+    chains = []
+    for copy in local:
+        copy.wait()
+    for sub in range(SUBS // 2):
+        chains.append([hop(1, sub)])
+    for copy in swap:
+        copy.wait()
+    for sub in range(SUBS // 2, SUBS):
+        chains.append([hop(1, sub)])
+
     lane = lax.broadcasted_iota(jnp.int32, (8, 128), 1)
     listed = jnp.zeros((8, 128), jnp.int32)
+    for copy in lists:
+        copy.wait()
     for t in range(16):
         listed = jnp.where(lane == t, owner_ref[t] * held + block_ref[t], listed)
     idx_v[0] = listed
-
-    pl.semaphore_wait(barrier, len(peers))
-    for copy in swap:
-        copy.start()
     idx_copy = remote(idx_v.at[0], idx_v.at[1], idx_send, idx_recv, sister)
     idx_copy.start()
-
-    rows = lax.broadcasted_iota(jnp.int32, (768, 768), 0)
-    want = (rows & 15) * BS + (rows >> 4)
-    perm[...] = (lax.broadcasted_iota(jnp.int32, (768, 768), 1) == want).astype(jnp.bfloat16)
-
-    for copy in local:
-        copy.wait()
-    for copy in swap:
-        copy.wait()
-
-    def ring(step):
-        ups, downs = lax.rem(z - (step - 1) + Z, Z), lax.rem(z + (step - 1), Z)
-        size = held if step == half else per
-        up = cg.at[pl.ds(ups * per, size)]
-        down = cg.at[pl.ds(downs * per + (per - size), size)]
-        return [
-            remote(up, up, ring_send.at[0, step - 1], ring_recv.at[0, step - 1], at_z(1)),
-            remote(down, down, ring_send.at[1, step - 1], ring_recv.at[1, step - 1], at_z(-1)),
-        ]
 
     def turn(part):
         rhs = tiles[:, :, part * 768:(part + 1) * 768].reshape(768, 768)
@@ -117,22 +137,27 @@
         lax.fori_loop(0, 3, body, 0)
 
     tt_copy = remote(tt.at[core], tt.at[core], tt_send, tt_recv, sister)
-    for step in range(1, half + 1):
-        copies = ring(step)
-        for copy in copies:
-            copy.start()
-        if step == 1:
-            tile_copy.wait()
-            for part in range(3):
-                turn(part)
-            tt_copy.start()
+    tile_copy.wait()
+    for part in range(3):
+        turn(part)
+    tt_copy.start()
+    for step in range(2, half + 1):
+        for sub in range(SUBS):
+            for copy in chains[sub][-1]:
+                copy.wait_recv()
+            chains[sub].append(hop(step, sub))
         if step == 2:
             idx_copy.wait()
             fetch = pltpu.make_async_copy(idx_v.at[1], idx_s, idx_sem)
             fetch.start()
             fetch.wait()
-        for copy in copies:
-            copy.wait()
+    for sub in range(SUBS):
+        for copy in chains[sub][-1]:
+            copy.wait_recv()
+    for chain in chains:
+        for copies in chain:
+            for copy in copies:
+                copy.wait_send()
     tt_copy.wait()
 
     for t in range(16):
@@ -224,13 +249,15 @@
         functools.partial(kernel, Y, Z, factor),
         out_shape=jax.ShapeDtypeStruct((1, 128), f32),
         in_specs=[
-            pl.BlockSpec(memory_space=pltpu.SMEM),
-            pl.BlockSpec(memory_space=pltpu.SMEM),
-            pl.BlockSpec(memory_space=pl.ANY),
-            pl.BlockSpec(memory_space=pl.ANY),
+            pl.BlockSpec(memory_space=pltpu.HBM),
+            pl.BlockSpec(memory_space=pltpu.HBM),
+            pl.BlockSpec(memory_space=pltpu.HBM),
+            pl.BlockSpec(memory_space=pltpu.HBM),
         ],
         out_specs=pl.BlockSpec(memory_space=pltpu.VMEM),
         scratch_shapes=[
+            pltpu.SMEM((count,), jnp.int32),
+            pltpu.SMEM((count,), jnp.int32),
             pltpu.VMEM((count, BS, BS * BS), bf),
             pltpu.VMEM((768, 768), bf),
             pltpu.VMEM((2, BS, BS, 768), bf),
@@ -246,14 +273,14 @@
             pltpu.VMEM((Y, 8, 128), f32),
             pltpu.VMEM((2, 8, 128), jnp.int32),
             pltpu.SMEM((8, 128), jnp.int32),
-            dma, dma((2,)), dma((2,)), dma((2,)),
-            dma((2, Z // 2)), dma((2, Z // 2)), dma, dma,
+            dma((2,)), dma, dma((2,)), dma((2,)), dma((2,)),
+            dma((2, Z // 2, SUBS)), dma((2, Z // 2, SUBS)), dma, dma,
             dma, dma, dma,
             dma((2, BS // PB)), dma((2, BS // PB)),
             dma((2 * X,)), dma((2 * X,)), dma((Y,)), dma((Y,)),
         ],
         compiler_params=pltpu.CompilerParams(
-            collective_id=0, has_side_effects=True, vmem_limit_bytes=48 * 1024 * 1024
+            collective_id=0, has_side_effects=True, vmem_limit_bytes=60 * 1024 * 1024
         ),
         name="exchange",
     )(tile_owner.reshape(count), tile_block, tile_values, coefficients)

time: 75.4 us -> 65.5 us (0.87)
  Pallas kernels: 70.4 us -> 64.2 us
  local copies, waits for them, and re-layouts: 4.82 us -> 1.19 us
    pallas_call x1, Pallas kernels: 70.4 us -> 64.2 us  [local(): pl.pallas_call(functools.partial(kernel, Y, Z, factor), out_shape=jax.Sha...]
    unnamed x9 -> x1, local copies, waits for them, and re-layouts: 4.82 us -> 1.19 us
where the time goes in v2:
time: 65.5 us; the launch traced here: 65.4 us
  Pallas kernels  64.2 us (98%)
  local copies, waits for them, and re-layouts  1.19 us (2%)
    pallas_call x1, Pallas kernels, local(): pl.pallas_call(functools.partial(kernel, Y, Z, factor), out_shape=jax.Sha...  64.2 us

profile of v2, /device:TPU:1, one launch (start us, length us, event | category | flops | bytes accessed | tf_op | source)
XLA Modules:
  0.0 65.4 jit_solution(15093734080931528855)
XLA Ops:
  0.0 64.2 %exchange.1 = f32[1,128]{1,0:T(1,128)} custom-call(s32[16]{0:T(128)} %bitcast.2, s32[16]{0:T(128)} %block_hbm.1, bf16[16,48,2304]{2,1,0:T(8,128)(2,1)} %tiles_ref.1, bf16[8,48,512]{2,1,0:T(8,128)(2,1)} %coef_ref.1), custom_call_target="tpu_custom_call" | custom-call | tf_op jit(solution)/shard_map/exchange/pallas_call | solution.py:248
  64.2 1.2 %copy.6 = f32[1,120]{1,0:T(1,128)} copy(f32[1,120]{1,0:T(1,128)} %bitcast.3) | data formatting | bytes 960

commit v3 on v2

--- a/solution.py
+++ b/solution.py
@@ -26,7 +26,7 @@
     owner_hbm, block_hbm, tiles_ref, coef_ref, out_ref,
     owner_ref, block_ref,
     tiles, perm, tt, cg, picked, occ, rsp, halo, band, send1, recv1, send2, recv2, idx_v, idx_s,
-    list_sem, tile_sem, coef_sem, sis_send, sis_recv, ring_send, ring_recv, tt_send, tt_recv,
+    list_sem, tile_sem, coef_sem, sis_send, sis_recv, ring_send, ring_recv, side_send, side_recv, tt_send, tt_recv,
     idx_send, idx_recv, idx_sem, halo_send, halo_recv, s1_send, s1_recv, s2_send, s2_recv,
 ):
     aux, ao = lax.axis_index("aux"), lax.axis_index("ao")
@@ -90,12 +90,30 @@
     for copy in swap:
         copy.start()
 
-    size = per // SUBS
+    size = held // SUBS
+    odd = x % 2
+
+    def piece(slot, sub):
+        part = lax.rem(sub // (SUBS // 2) + core, 2)
+        start = part * held + odd * (held // 2) + sub % (SUBS // 2) * size
+        return cg.at[pl.ds(lax.rem(slot + Z, Z) * per + start, size)]
+
+    def beside(sub):
+        part = lax.rem(sub // (SUBS // 2) + core, 2)
+        step = (1 - 2 * odd) * (1 - 2 * part)
+        return {"aux": y * X + lax.rem(x + step + X, X), "ao": ao}
+
+    def share(step, sub):
+        slots = [z - step, z + step] if step < half else [z + step]
+        copies = []
+        for i, slot in enumerate(slots):
+            ref = piece(slot, sub)
+            copies.append(remote(ref, ref, side_send.at[i, step - 1, sub], side_recv.at[i, step - 1, sub], beside(sub)))
+            copies[-1].start()
+        return copies
 
     def hop(step, sub):
-        spot_in = lax.rem(sub + core * (SUBS // 2), SUBS) * size
-        ups, downs = lax.rem(z - (step - 1) + Z, Z), lax.rem(z + (step - 1), Z)
-        up, down = cg.at[pl.ds(ups * per + spot_in, size)], cg.at[pl.ds(downs * per + spot_in, size)]
+        up, down = piece(z - (step - 1), sub), piece(z + (step - 1), sub)
         copies = []
         if step < half or sub % 2 == 0:
             copies.append(remote(up, up, ring_send.at[0, step - 1, sub], ring_recv.at[0, step - 1, sub], at_z(1)))
@@ -141,11 +159,13 @@
     for part in range(3):
         turn(part)
     tt_copy.start()
+    sides = []
     for step in range(2, half + 1):
         for sub in range(SUBS):
             for copy in chains[sub][-1]:
                 copy.wait_recv()
             chains[sub].append(hop(step, sub))
+            sides += share(step - 1, sub)
         if step == 2:
             idx_copy.wait()
             fetch = pltpu.make_async_copy(idx_v.at[1], idx_s, idx_sem)
@@ -154,6 +174,11 @@
     for sub in range(SUBS):
         for copy in chains[sub][-1]:
             copy.wait_recv()
+        sides += share(half, sub)
+    for copy in sides:
+        copy.wait_recv()
+    for copy in sides:
+        copy.wait_send()
     for chain in chains:
         for copies in chain:
             for copy in copies:
@@ -274,7 +299,7 @@
             pltpu.VMEM((2, 8, 128), jnp.int32),
             pltpu.SMEM((8, 128), jnp.int32),
             dma((2,)), dma, dma((2,)), dma((2,)), dma((2,)),
-            dma((2, Z // 2, SUBS)), dma((2, Z // 2, SUBS)), dma, dma,
+            dma((2, Z // 2, SUBS)), dma((2, Z // 2, SUBS)), dma((2, Z // 2, SUBS)), dma((2, Z // 2, SUBS)), dma, dma,
             dma, dma, dma,
             dma((2, BS // PB)), dma((2, BS // PB)),
             dma((2 * X,)), dma((2 * X,)), dma((Y,)), dma((Y,)),

time: 65.5 us -> 58.1 us (0.89)
  Pallas kernels: 64.2 us -> 56.8 us
    pallas_call x1, Pallas kernels: 64.2 us -> 56.8 us  [local(): pl.pallas_call(functools.partial(kernel, Y, Z, factor), out_shape=jax.Sha...]
where the time goes in v3:
time: 58.1 us; the launch traced here: 58 us
  Pallas kernels  56.8 us (98%)
  local copies, waits for them, and re-layouts  1.19 us (2%)
    pallas_call x1, Pallas kernels, local(): pl.pallas_call(functools.partial(kernel, Y, Z, factor), out_shape=jax.Sha...  56.8 us
    unnamed x1, local copies, waits for them, and re-layouts  1.19 us

profile of v3, /device:TPU:1, one launch (start us, length us, event | category | flops | bytes accessed | tf_op | source)
XLA Modules:
  0.0 58.0 jit_solution(5193743726929794148)
XLA Ops:
  0.0 56.8 %exchange.1 = f32[1,128]{1,0:T(1,128)} custom-call(s32[16]{0:T(128)} %bitcast.2, s32[16]{0:T(128)} %block_hbm.1, bf16[16,48,2304]{2,1,0:T(8,128)(2,1)} %tiles_ref.1, bf16[8,48,512]{2,1,0:T(8,128)(2,1)} %coef_ref.1), custom_call_target="tpu_custom_call" | custom-call | tf_op jit(solution)/shard_map/exchange/pallas_call | solution.py:273
  56.8 1.2 %copy.6 = f32[1,120]{1,0:T(1,128)} copy(f32[1,120]{1,0:T(1,128)} %bitcast.3) | data formatting | bytes 960

commit v4 on v3

--- a/solution.py
+++ b/solution.py
@@ -25,8 +25,8 @@
     Y, Z, factor,
     owner_hbm, block_hbm, tiles_ref, coef_ref, out_ref,
     owner_ref, block_ref,
-    tiles, perm, tt, cg, picked, occ, rsp, halo, band, send1, recv1, send2, recv2, idx_v, idx_s,
-    list_sem, tile_sem, coef_sem, sis_send, sis_recv, ring_send, ring_recv, side_send, side_recv, tt_send, tt_recv,
+    tiles, perm, tt, cg, picked, occ, rsp, halo, band, parts, cross_in, rows_out, rows_in, idx_v, idx_s,
+    list_sem, tile_sem, coef_sem, sis_send, sis_recv, ring_send, ring_recv, side_send, side_recv, far_send, far_recv, tt_send, tt_recv,
     idx_send, idx_recv, idx_sem, halo_send, halo_recv, s1_send, s1_recv, s2_send, s2_recv,
 ):
     aux, ao = lax.axis_index("aux"), lax.axis_index("ao")
@@ -36,18 +36,14 @@
     held = coef_ref.shape[0]
     per = 2 * held
     half = Z // 2
-    group = 2 * X
-    spot = x * 2 + core
+    plane = [(dx, dy) for dx in range(X) for dy in range(Y) if dx or dy]
+    plane.sort(key=lambda at: -(min(at[0], X - at[0]) + min(at[1], Y - at[1])))
 
     def at_z(step):
         return {"aux": aux, "ao": lax.rem(z + step + Z, Z) * 2 + core}
 
-    def at_group(step):
-        there = lax.rem(spot + step, group)
-        return {"aux": y * X + there // 2, "ao": z * 2 + there % 2}
-
-    def at_y(step):
-        return {"aux": lax.rem(y + step, Y) * X + x, "ao": ao}
+    def at_plane(dx, dy):
+        return {"aux": lax.rem(y + dy, Y) * X + lax.rem(x + dx, X), "ao": ao}
 
     sister = {"aux": aux, "ao": z * 2 + other}
 
@@ -67,7 +63,7 @@
         copy.start()
 
     barrier = pltpu.get_barrier_semaphore()
-    peers = [at_z(1), at_z(-1)] + [at_group(d) for d in range(1, group)] + [at_y(d) for d in range(1, Y)]
+    peers = [at_plane(dx, dy) for dx, dy in plane] + [at_z(half), at_z(1), at_z(-1), sister]
     for peer in peers:
         pl.semaphore_signal(barrier, inc=1, device_id=peer, device_id_type=pl.DeviceIdType.MESH)
 
@@ -114,14 +110,17 @@
 
     def hop(step, sub):
         up, down = piece(z - (step - 1), sub), piece(z + (step - 1), sub)
-        copies = []
-        if step < half or sub % 2 == 0:
-            copies.append(remote(up, up, ring_send.at[0, step - 1, sub], ring_recv.at[0, step - 1, sub], at_z(1)))
-        if step < half or sub % 2 == 1:
-            copies.append(remote(down, down, ring_send.at[1, step - 1, sub], ring_recv.at[1, step - 1, sub], at_z(-1)))
+        copies = [
+            remote(up, up, ring_send.at[0, step - 1, sub], ring_recv.at[0, step - 1, sub], at_z(1)),
+            remote(down, down, ring_send.at[1, step - 1, sub], ring_recv.at[1, step - 1, sub], at_z(-1)),
+        ]
         for copy in copies:
             copy.start()
         return copies
+
+    def eighth(slot):
+        start = y // (Y // 2) * held + odd * (held // 2) + y % (Y // 2)
+        return cg.at[pl.ds(lax.rem(slot + Z, Z) * per + start, 1)]
 
     chains = []
     for copy in local:
@@ -130,6 +129,8 @@
         chains.append([hop(1, sub)])
     for copy in swap:
         copy.wait()
+    far = remote(eighth(z), eighth(z), far_send.at[0], far_recv.at[0], at_z(half))
+    far.start()
     for sub in range(SUBS // 2, SUBS):
         chains.append([hop(1, sub)])
 
@@ -154,36 +155,53 @@
 
         lax.fori_loop(0, 3, body, 0)
 
-    tt_copy = remote(tt.at[core], tt.at[core], tt_send, tt_recv, sister)
-    tile_copy.wait()
-    for part in range(3):
+    turned = []
+
+    def turn_next():
+        part = len(turned)
         turn(part)
-    tt_copy.start()
-    sides = []
-    for step in range(2, half + 1):
+        ref = tt.at[core, :, part * 16:(part + 1) * 16]
+        turned.append(remote(ref, ref, tt_send.at[part], tt_recv.at[part], sister))
+        turned[-1].start()
+
+    sides, rounds = [], []
+    for step in range(2, half):
         for sub in range(SUBS):
             for copy in chains[sub][-1]:
                 copy.wait_recv()
             chains[sub].append(hop(step, sub))
             sides += share(step - 1, sub)
         if step == 2:
-            idx_copy.wait()
-            fetch = pltpu.make_async_copy(idx_v.at[1], idx_s, idx_sem)
-            fetch.start()
-            fetch.wait()
+            far.wait_recv()
+            ref = eighth(z + half)
+            for dy in sorted(range(1, Y), key=lambda dy: -min(dy, Y - dy)):
+                rounds.append(remote(ref, ref, far_send.at[dy], far_recv.at[dy], at_plane(0, dy)))
+                rounds[-1].start()
+            tile_copy.wait()
+        turn_next()
+    idx_copy.wait()
+    fetch = pltpu.make_async_copy(idx_v.at[1], idx_s, idx_sem)
+    fetch.start()
+    turn_next()
+    for copy in rounds:
+        copy.wait_recv()
+    for sub in range(SUBS):
+        sides += share(half, sub)
     for sub in range(SUBS):
         for copy in chains[sub][-1]:
             copy.wait_recv()
-        sides += share(half, sub)
+        sides += share(half - 1, sub)
+    fetch.wait()
+    for copy in turned:
+        copy.wait()
     for copy in sides:
         copy.wait_recv()
-    for copy in sides:
+    for copy in sides + rounds + [far]:
         copy.wait_send()
     for chain in chains:
         for copies in chain:
             for copy in copies:
                 copy.wait_send()
-    tt_copy.wait()
 
     for t in range(16):
         picked[core, t * BS:(t + 1) * BS, :] = cg[owner_ref[t] * held + block_ref[t]]
@@ -227,39 +245,35 @@
     )
     band[...] = jnp.where(outside, 0.0, total)
 
-    for there in range(group):
-        xx, c = there // 2, there % 2
-        first = c * BS + 3 * (xx // 2)
-        shift = BS * c
-        if xx % 2 == 0:
-            one, two = band[pl.ds(first, 8, stride=6), :], band[pl.ds(first + 1, 8, stride=6), :]
-            a, b, cut = (128 - shift) % 128, (80 - shift) % 128, 80
-        else:
-            one, two = band[pl.ds(first + 1, 8, stride=6), :], band[pl.ds(first + 2, 8, stride=6), :]
-            a, b, cut = (128 - shift - 40) % 128, (40 - shift) % 128, 40
-        one = pltpu.roll(one, a, 1) if a else one
-        two = pltpu.roll(two, b, 1) if b else two
-        send1[there] = jnp.where(lane < cut, one, two)
-
+    for xx in range(X):
+        for c in range(2):
+            first = c * BS + 3 * (xx // 2)
+            shift = BS * c
+            if xx % 2 == 0:
+                one, two = band[pl.ds(first, 8, stride=6), :], band[pl.ds(first + 1, 8, stride=6), :]
+                a, b, cut = (128 - shift) % 128, (80 - shift) % 128, 80
+            else:
+                one, two = band[pl.ds(first + 1, 8, stride=6), :], band[pl.ds(first + 2, 8, stride=6), :]
+                a, b, cut = (128 - shift - 40) % 128, (40 - shift) % 128, 40
+            one = pltpu.roll(one, a, 1) if a else one
+            two = pltpu.roll(two, b, 1) if b else two
+            parts[c, xx] = jnp.where(lane < cut, one, two)
+
+    cross = remote(parts.at[other], cross_in, s1_send, s1_recv, sister)
+    cross.start()
+    cross.wait()
+    rows_out[...] = (parts[core] + cross_in[...]).reshape(X * Y, 1, 128)
     copies = []
-    for d in range(1, group):
-        there = lax.rem(spot + d, group)
-        copies.append(remote(send1.at[there], recv1.at[d], s1_send.at[d], s1_recv.at[d], at_group(d)))
+    for i, (dx, dy) in enumerate(plane):
+        there = lax.rem(x + dx, X) * Y + lax.rem(y + dy, Y)
+        copies.append(remote(rows_out.at[there], rows_in.at[i], s2_send.at[i], s2_recv.at[i], at_plane(dx, dy)))
         copies[-1].start()
-    partial = send1[spot]
-    for d in range(1, group):
-        copies[d - 1].wait()
-        partial = partial + recv1[d]
-    send2[...] = partial
-    copies = []
-    for d in range(1, Y):
-        copies.append(remote(send2, recv2.at[d], s2_send.at[d], s2_recv.at[d], at_y(d)))
-        copies[-1].start()
-    for d in range(1, Y):
-        copies[d - 1].wait()
-        partial = partial + recv2[d]
-    row = lax.broadcasted_iota(jnp.int32, (8, 128), 0)
-    out_ref[...] = jnp.sum(jnp.where(row == y, partial, 0.0), axis=0, keepdims=True) * factor
+    rows_in[X * Y - 1] = rows_out[x * Y + y]
+    for copy in copies:
+        copy.wait_recv()
+    out_ref[...] = jnp.sum(rows_in[...], axis=0) * factor
+    for copy in copies:
+        copy.wait_send()
 
 
 def local(tile_values, tile_owner, tile_block, coefficients):
@@ -292,17 +306,17 @@
             pltpu.VMEM((BS, 2 * BS, 128), bf),
             pltpu.VMEM((2, BS, HW, 128), bf),
             pltpu.VMEM((2 * BS, 2 * BS + 2 * HW), f32),
-            pltpu.VMEM((2 * X, 8, 128), f32),
-            pltpu.VMEM((2 * X, 8, 128), f32),
-            pltpu.VMEM((8, 128), f32),
-            pltpu.VMEM((Y, 8, 128), f32),
+            pltpu.VMEM((2, X, 8, 128), f32),
+            pltpu.VMEM((X, 8, 128), f32),
+            pltpu.VMEM((X * Y, 1, 128), f32),
+            pltpu.VMEM((X * Y, 1, 128), f32),
             pltpu.VMEM((2, 8, 128), jnp.int32),
             pltpu.SMEM((8, 128), jnp.int32),
             dma((2,)), dma, dma((2,)), dma((2,)), dma((2,)),
-            dma((2, Z // 2, SUBS)), dma((2, Z // 2, SUBS)), dma((2, Z // 2, SUBS)), dma((2, Z // 2, SUBS)), dma, dma,
+            dma((2, Z // 2, SUBS)), dma((2, Z // 2, SUBS)), dma((2, Z // 2, SUBS)), dma((2, Z // 2, SUBS)), dma((Y,)), dma((Y,)), dma((3,)), dma((3,)),
             dma, dma, dma,
             dma((2, BS // PB)), dma((2, BS // PB)),
-            dma((2 * X,)), dma((2 * X,)), dma((Y,)), dma((Y,)),
+            dma, dma, dma((X * Y,)), dma((X * Y,)),
         ],
         compiler_params=pltpu.CompilerParams(
             collective_id=0, has_side_effects=True, vmem_limit_bytes=60 * 1024 * 1024

time: 58.1 us -> 55.6 us (0.957)
  Pallas kernels: 56.8 us -> 54.3 us
    pallas_call x1, Pallas kernels: 56.8 us -> 54.3 us  [local(): pl.pallas_call(functools.partial(kernel, Y, Z, factor), out_shape=jax.Sha...]
where the time goes in v4:
time: 55.6 us; the launch traced here: 55.5 us
  Pallas kernels  54.3 us (98%)
  local copies, waits for them, and re-layouts  1.19 us (2%)
    pallas_call x1, Pallas kernels, local(): pl.pallas_call(functools.partial(kernel, Y, Z, factor), out_shape=jax.Sha...  54.3 us
    unnamed x1, local copies, waits for them, and re-layouts  1.19 us

profile of v4, /device:TPU:1, one launch (start us, length us, event | category | flops | bytes accessed | tf_op | source)
XLA Modules:
  0.0 55.5 jit_solution(16283167333487548814)
XLA Ops:
  0.0 54.3 %exchange.1 = f32[1,128]{1,0:T(1,128)} custom-call(s32[16]{0:T(128)} %bitcast.2, s32[16]{0:T(128)} %block_hbm.1, bf16[16,48,2304]{2,1,0:T(8,128)(2,1)} %tiles_ref.1, bf16[8,48,512]{2,1,0:T(8,128)(2,1)} %coef_ref.1), custom_call_target="tpu_custom_call" | custom-call | tf_op jit(solution)/shard_map/exchange/pallas_call | solution.py:287
  54.3 1.2 %copy.6 = f32[1,120]{1,0:T(1,128)} copy(f32[1,120]{1,0:T(1,128)} %bitcast.3) | data formatting | bytes 960

commit v5 on v4

--- a/solution.py
+++ b/solution.py
@@ -11,7 +11,7 @@
 X = 4
 BS = 48
 HW = 16
-PB = 8
+PB = 16
 SUBS = 4
 NN = (((1,), (0,)), ((), ()))
 NT = (((1,), (1,)), ((), ()))
@@ -27,7 +27,7 @@
     owner_ref, block_ref,
     tiles, perm, tt, cg, picked, occ, rsp, halo, band, parts, cross_in, rows_out, rows_in, idx_v, idx_s,
     list_sem, tile_sem, coef_sem, sis_send, sis_recv, ring_send, ring_recv, side_send, side_recv, far_send, far_recv, tt_send, tt_recv,
-    idx_send, idx_recv, idx_sem, halo_send, halo_recv, s1_send, s1_recv, s2_send, s2_recv,
+    idx_send, idx_recv, idx_sem, halo_send, halo_recv, s1_send, s1_recv, s2_send, s2_recv, known,
 ):
     aux, ao = lax.axis_index("aux"), lax.axis_index("ao")
     y, x = aux // X, aux % X
@@ -53,20 +53,6 @@
             device_id=where, device_id_type=pl.DeviceIdType.MESH,
         )
 
-    tile_copy = pltpu.make_async_copy(tiles_ref, tiles, tile_sem)
-    tile_copy.start()
-    lists = [
-        pltpu.make_async_copy(owner_hbm, owner_ref, list_sem.at[0]),
-        pltpu.make_async_copy(block_hbm, block_ref, list_sem.at[1]),
-    ]
-    for copy in lists:
-        copy.start()
-
-    barrier = pltpu.get_barrier_semaphore()
-    peers = [at_plane(dx, dy) for dx, dy in plane] + [at_z(half), at_z(1), at_z(-1), sister]
-    for peer in peers:
-        pl.semaphore_signal(barrier, inc=1, device_id=peer, device_id_type=pl.DeviceIdType.MESH)
-
     mine = ao * held
     local, swap = [], []
     for part in range(2):
@@ -78,16 +64,32 @@
     for copy in local:
         copy.start()
 
-    rows = lax.broadcasted_iota(jnp.int32, (768, 768), 0)
-    want = (rows & 15) * BS + (rows >> 4)
-    perm[...] = (lax.broadcasted_iota(jnp.int32, (768, 768), 1) == want).astype(jnp.bfloat16)
-
+    tile_copy = pltpu.make_async_copy(tiles_ref, tiles, tile_sem)
+    lists = [
+        pltpu.make_async_copy(owner_hbm, owner_ref, list_sem.at[0]),
+        pltpu.make_async_copy(block_hbm, block_ref, list_sem.at[1]),
+    ]
+    for copy in lists + [tile_copy]:
+        copy.start()
+
+    barrier = pltpu.get_barrier_semaphore()
+    y_near, y_next = [at_plane(0, 1), at_plane(0, Y - 1)], [at_plane(0, 2), at_plane(0, Y - 2)]
+    x_near = [at_plane(1, 0), at_plane(X - 1, 0)]
+    y_ring = [at_plane(0, dy) for dy in range(1, Y)]
+    peers = [sister, at_z(1), at_z(-1), at_z(half)] + x_near + y_near
+
+    def tell(which, whom):
+        for peer in whom:
+            pl.semaphore_signal(known.at[which], inc=1, device_id=peer, device_id_type=pl.DeviceIdType.MESH)
+
+    for peer in peers:
+        pl.semaphore_signal(barrier, inc=1, device_id=peer, device_id_type=pl.DeviceIdType.MESH)
     pl.semaphore_wait(barrier, len(peers))
     for copy in swap:
         copy.start()
 
     size = held // SUBS
-    odd = x % 2
+    odd = lax.rem(x + y, 2)
 
     def piece(slot, sub):
         part = lax.rem(sub // (SUBS // 2) + core, 2)
@@ -95,32 +97,36 @@
         return cg.at[pl.ds(lax.rem(slot + Z, Z) * per + start, size)]
 
     def beside(sub):
-        part = lax.rem(sub // (SUBS // 2) + core, 2)
-        step = (1 - 2 * odd) * (1 - 2 * part)
-        return {"aux": y * X + lax.rem(x + step + X, X), "ao": ao}
+        step = (1 - 2 * odd) * (1 - 2 * (sub // 2))
+        return at_plane(step + X, 0) if sub % 2 == 0 else at_plane(0, step + Y)
+
+    started = []
+
+    def go(copies):
+        for copy in copies:
+            copy.start()
+        started.extend(copies)
+        return copies
 
     def share(step, sub):
         slots = [z - step, z + step] if step < half else [z + step]
-        copies = []
-        for i, slot in enumerate(slots):
-            ref = piece(slot, sub)
-            copies.append(remote(ref, ref, side_send.at[i, step - 1, sub], side_recv.at[i, step - 1, sub], beside(sub)))
-            copies[-1].start()
-        return copies
+        refs = [piece(slot, sub) for slot in slots]
+        return go([
+            remote(ref, ref, side_send.at[i, step - 1, sub], side_recv.at[i, step - 1, sub], beside(sub))
+            for i, ref in enumerate(refs)
+        ])
 
     def hop(step, sub):
-        up, down = piece(z - (step - 1), sub), piece(z + (step - 1), sub)
-        copies = [
-            remote(up, up, ring_send.at[0, step - 1, sub], ring_recv.at[0, step - 1, sub], at_z(1)),
-            remote(down, down, ring_send.at[1, step - 1, sub], ring_recv.at[1, step - 1, sub], at_z(-1)),
-        ]
-        for copy in copies:
-            copy.start()
-        return copies
-
-    def eighth(slot):
-        start = y // (Y // 2) * held + odd * (held // 2) + y % (Y // 2)
-        return cg.at[pl.ds(lax.rem(slot + Z, Z) * per + start, 1)]
+        refs = [piece(z - (step - 1), sub), piece(z + (step - 1), sub)]
+        return go([
+            remote(ref, ref, ring_send.at[i, step - 1, sub], ring_recv.at[i, step - 1, sub], at_z(1 - 2 * i))
+            for i, ref in enumerate(refs)
+        ])
+
+    def fourth(slot):
+        at = y // 2
+        start = at // 2 * held + odd * (held // 2) + at % 2 * 2
+        return cg.at[pl.ds(lax.rem(slot + Z, Z) * per + start, 2)]
 
     chains = []
     for copy in local:
@@ -129,7 +135,7 @@
         chains.append([hop(1, sub)])
     for copy in swap:
         copy.wait()
-    far = remote(eighth(z), eighth(z), far_send.at[0], far_recv.at[0], at_z(half))
+    far = remote(fourth(z), fourth(z), far_send.at[0], far_recv.at[0], at_z(half))
     far.start()
     for sub in range(SUBS // 2, SUBS):
         chains.append([hop(1, sub)])
@@ -143,6 +149,12 @@
     idx_v[0] = listed
     idx_copy = remote(idx_v.at[0], idx_v.at[1], idx_send, idx_recv, sister)
     idx_copy.start()
+    tell(0, y_near)
+    tell(1, x_near)
+
+    rows = lax.broadcasted_iota(jnp.int32, (768, 768), 0)
+    want = (rows & 15) * BS + (rows >> 4)
+    perm[...] = (lax.broadcasted_iota(jnp.int32, (768, 768), 1) == want).astype(jnp.bfloat16)
 
     def turn(part):
         rhs = tiles[:, :, part * 768:(part + 1) * 768].reshape(768, 768)
@@ -165,6 +177,8 @@
         turned[-1].start()
 
     sides, rounds = [], []
+    pl.semaphore_wait(known.at[0], 2)
+    tell(2, y_next)
     for step in range(2, half):
         for sub in range(SUBS):
             for copy in chains[sub][-1]:
@@ -173,10 +187,13 @@
             sides += share(step - 1, sub)
         if step == 2:
             far.wait_recv()
-            ref = eighth(z + half)
-            for dy in sorted(range(1, Y), key=lambda dy: -min(dy, Y - dy)):
+            pl.semaphore_wait(known.at[2], 2)
+            ref = fourth(z + half)
+            for dy in (4, 2, 6):
                 rounds.append(remote(ref, ref, far_send.at[dy], far_recv.at[dy], at_plane(0, dy)))
                 rounds[-1].start()
+            pl.semaphore_wait(known.at[1], 2)
+            tell(3, y_ring)
             tile_copy.wait()
         turn_next()
     idx_copy.wait()
@@ -196,12 +213,8 @@
         copy.wait()
     for copy in sides:
         copy.wait_recv()
-    for copy in sides + rounds + [far]:
+    for copy in started + rounds + [far]:
         copy.wait_send()
-    for chain in chains:
-        for copies in chain:
-            for copy in copies:
-                copy.wait_send()
 
     for t in range(16):
         picked[core, t * BS:(t + 1) * BS, :] = cg[owner_ref[t] * held + block_ref[t]]
@@ -213,15 +226,10 @@
         for r in range(2):
             right = picked[r]
 
-            def body(i, carry):
-                p = b * PB + i * 8
-                got = dot(tt[r, pl.ds(p, 8)].reshape(8 * BS, 768), right, NN).astype(jnp.bfloat16)
-                got = got.reshape(8, BS, 256)
-                occ[pl.ds(p, 8), r * BS:(r + 1) * BS, :] = got[:, :, :128]
-                rsp[pl.ds(p, 8), r * BS:(r + 1) * BS, :] = got[:, :, 128:]
-                return carry
-
-            lax.fori_loop(0, PB // 8, body, 0)
+            got = dot(tt[r, ps].reshape(PB * BS, 768), right, NN).astype(jnp.bfloat16)
+            got = got.reshape(PB, BS, 256)
+            occ[ps, r * BS:(r + 1) * BS, :] = got[:, :, :128]
+            rsp[ps, r * BS:(r + 1) * BS, :] = got[:, :, 128:]
         down = remote(rsp.at[ps, 0:HW], halo.at[1, ps], halo_send.at[1, b], halo_recv.at[1, b], at_z(-1))
         up = remote(rsp.at[ps, 2 * BS - HW:2 * BS], halo.at[0, ps], halo_send.at[0, b], halo_recv.at[0, b], at_z(1))
         down.start()
@@ -262,6 +270,7 @@
     cross = remote(parts.at[other], cross_in, s1_send, s1_recv, sister)
     cross.start()
     cross.wait()
+    pl.semaphore_wait(known.at[3], Y - 1)
     rows_out[...] = (parts[core] + cross_in[...]).reshape(X * Y, 1, 128)
     copies = []
     for i, (dx, dy) in enumerate(plane):
@@ -317,6 +326,7 @@
             dma, dma, dma,
             dma((2, BS // PB)), dma((2, BS // PB)),
             dma, dma, dma((X * Y,)), dma((X * Y,)),
+            pltpu.SemaphoreType.REGULAR((4,)),
         ],
         compiler_params=pltpu.CompilerParams(
             collective_id=0, has_side_effects=True, vmem_limit_bytes=60 * 1024 * 1024

time: 55.6 us -> 55.1 us (level)
  no operation moved by 1% of the time
where the time goes in v5:
time: 55.1 us; the launch traced here: 55 us
  Pallas kernels  53.8 us (98%)
  local copies, waits for them, and re-layouts  1.19 us (2%)
    pallas_call x1, Pallas kernels, local(): pl.pallas_call(functools.partial(kernel, Y, Z, factor), out_shape=jax.Sha...  53.8 us
    unnamed x1, local copies, waits for them, and re-layouts  1.19 us

profile of v5, /device:TPU:1, one launch (start us, length us, event | category | flops | bytes accessed | tf_op | source)
XLA Modules:
  0.0 55.0 jit_solution(4444015546729361022)
XLA Ops:
  0.0 53.8 %exchange.1 = f32[1,128]{1,0:T(1,128)} custom-call(s32[16]{0:T(128)} %bitcast.2, s32[16]{0:T(128)} %block_hbm.1, bf16[16,48,2304]{2,1,0:T(8,128)(2,1)} %tiles_ref.1, bf16[8,48,512]{2,1,0:T(8,128)(2,1)} %coef_ref.1), custom_call_target="tpu_custom_call" | custom-call | tf_op jit(solution)/shard_map/exchange/pallas_call | solution.py:296
  53.8 1.2 %copy.6 = f32[1,120]{1,0:T(1,128)} copy(f32[1,120]{1,0:T(1,128)} %bitcast.3) | data formatting | bytes 960

commit v6 on v5

--- a/solution.py
+++ b/solution.py
@@ -134,7 +134,7 @@
     for sub in range(SUBS // 2):
         chains.append([hop(1, sub)])
     for copy in swap:
-        copy.wait()
+        copy.wait_recv()
     far = remote(fourth(z), fourth(z), far_send.at[0], far_recv.at[0], at_z(half))
     far.start()
     for sub in range(SUBS // 2, SUBS):
@@ -196,7 +196,7 @@
             tell(3, y_ring)
             tile_copy.wait()
         turn_next()
-    idx_copy.wait()
+    idx_copy.wait_recv()
     fetch = pltpu.make_async_copy(idx_v.at[1], idx_s, idx_sem)
     fetch.start()
     turn_next()
@@ -210,11 +210,9 @@
         sides += share(half - 1, sub)
     fetch.wait()
     for copy in turned:
-        copy.wait()
+        copy.wait_recv()
     for copy in sides:
         copy.wait_recv()
-    for copy in started + rounds + [far]:
-        copy.wait_send()
 
     for t in range(16):
         picked[core, t * BS:(t + 1) * BS, :] = cg[owner_ref[t] * held + block_ref[t]]
@@ -239,7 +237,7 @@
     total = jnp.zeros((2 * BS, 2 * BS + 2 * HW), jnp.float32)
     for b in range(BS // PB):
         for copy in halos[b]:
-            copy.wait()
+            copy.wait_recv()
         left, wide = [], []
         for p in range(b * PB, (b + 1) * PB):
             left.append(occ[p])
@@ -269,7 +267,7 @@
 
     cross = remote(parts.at[other], cross_in, s1_send, s1_recv, sister)
     cross.start()
-    cross.wait()
+    cross.wait_recv()
     pl.semaphore_wait(known.at[3], Y - 1)
     rows_out[...] = (parts[core] + cross_in[...]).reshape(X * Y, 1, 128)
     copies = []
@@ -281,7 +279,9 @@
     for copy in copies:
         copy.wait_recv()
     out_ref[...] = jnp.sum(rows_in[...], axis=0) * factor
-    for copy in copies:
+    for pair in halos:
+        copies += pair
+    for copy in swap + turned + started + rounds + copies + [idx_copy, far, cross]:
         copy.wait_send()
 
 

time: 55.1 us -> 55.1 us (level)
  no operation moved by 1% of the time
where the time goes in v6:
time: 55.1 us; the launch traced here: 55 us
  Pallas kernels  53.8 us (98%)
  local copies, waits for them, and re-layouts  1.19 us (2%)
    pallas_call x1, Pallas kernels, local(): pl.pallas_call(functools.partial(kernel, Y, Z, factor), out_shape=jax.Sha...  53.8 us
    unnamed x1, local copies, waits for them, and re-layouts  1.19 us

profile of v6, /device:TPU:1, one launch (start us, length us, event | category | flops | bytes accessed | tf_op | source)
XLA Modules:
  0.0 55.0 jit_solution(5707948577805245795)
XLA Ops:
  0.0 53.8 %exchange.1 = f32[1,128]{1,0:T(1,128)} custom-call(s32[16]{0:T(128)} %bitcast.2, s32[16]{0:T(128)} %block_hbm.1, bf16[16,48,2304]{2,1,0:T(8,128)(2,1)} %tiles_ref.1, bf16[8,48,512]{2,1,0:T(8,128)(2,1)} %coef_ref.1), custom_call_target="tpu_custom_call" | custom-call | tf_op jit(solution)/shard_map/exchange/pallas_call | solution.py:296
  53.8 1.2 %copy.6 = f32[1,120]{1,0:T(1,128)} copy(f32[1,120]{1,0:T(1,128)} %bitcast.3) | data formatting | bytes 960

commit v7 on v6

--- a/solution.py
+++ b/solution.py
@@ -11,7 +11,7 @@
 X = 4
 BS = 48
 HW = 16
-PB = 16
+PB = 8
 SUBS = 4
 NN = (((1,), (0,)), ((), ()))
 NT = (((1,), (1,)), ((), ()))

time: 55.1 us -> 54.9 us (level)
  no operation moved by 1% of the time
where the time goes in v7:
time: 54.9 us; the launch traced here: 54.8 us
  Pallas kernels  53.6 us (98%)
  local copies, waits for them, and re-layouts  1.19 us (2%)
    pallas_call x1, Pallas kernels, local(): pl.pallas_call(functools.partial(kernel, Y, Z, factor), out_shape=jax.Sha...  53.6 us
    unnamed x1, local copies, waits for them, and re-layouts  1.19 us

profile of v7, /device:TPU:1, one launch (start us, length us, event | category | flops | bytes accessed | tf_op | source)
XLA Modules:
  0.0 54.8 jit_solution(12546648458744779405)
XLA Ops:
  0.0 53.6 %exchange.1 = f32[1,128]{1,0:T(1,128)} custom-call(s32[16]{0:T(128)} %bitcast.2, s32[16]{0:T(128)} %block_hbm.1, bf16[16,48,2304]{2,1,0:T(8,128)(2,1)} %tiles_ref.1, bf16[8,48,512]{2,1,0:T(8,128)(2,1)} %coef_ref.1), custom_call_target="tpu_custom_call" | custom-call | tf_op jit(solution)/shard_map/exchange/pallas_call | solution.py:296
  53.6 1.2 %copy.6 = f32[1,120]{1,0:T(1,128)} copy(f32[1,120]{1,0:T(1,128)} %bitcast.3) | data formatting | bytes 960

commit v8 on v7

--- a/solution.py
+++ b/solution.py
@@ -179,6 +179,8 @@
     sides, rounds = [], []
     pl.semaphore_wait(known.at[0], 2)
     tell(2, y_next)
+    tile_copy.wait()
+    turn_next()
     for step in range(2, half):
         for sub in range(SUBS):
             for copy in chains[sub][-1]:
@@ -194,12 +196,10 @@
                 rounds[-1].start()
             pl.semaphore_wait(known.at[1], 2)
             tell(3, y_ring)
-            tile_copy.wait()
         turn_next()
     idx_copy.wait_recv()
     fetch = pltpu.make_async_copy(idx_v.at[1], idx_s, idx_sem)
     fetch.start()
-    turn_next()
     for copy in rounds:
         copy.wait_recv()
     for sub in range(SUBS):

time: 54.9 us -> 54.9 us (level)
  no operation moved by 1% of the time
where the time goes in v8:
time: 54.9 us; the launch traced here: 54.8 us
  Pallas kernels  53.6 us (98%)
  local copies, waits for them, and re-layouts  1.19 us (2%)
    pallas_call x1, Pallas kernels, local(): pl.pallas_call(functools.partial(kernel, Y, Z, factor), out_shape=jax.Sha...  53.6 us
    unnamed x1, local copies, waits for them, and re-layouts  1.19 us

profile of v8, /device:TPU:1, one launch (start us, length us, event | category | flops | bytes accessed | tf_op | source)
XLA Modules:
  0.0 54.8 jit_solution(13612325337166234135)
XLA Ops:
  0.0 53.6 %exchange.1 = f32[1,128]{1,0:T(1,128)} custom-call(s32[16]{0:T(128)} %bitcast.2, s32[16]{0:T(128)} %block_hbm.1, bf16[16,48,2304]{2,1,0:T(8,128)(2,1)} %tiles_ref.1, bf16[8,48,512]{2,1,0:T(8,128)(2,1)} %coef_ref.1), custom_call_target="tpu_custom_call" | custom-call | tf_op jit(solution)/shard_map/exchange/pallas_call | solution.py:296
  53.6 1.2 %copy.6 = f32[1,120]{1,0:T(1,128)} copy(f32[1,120]{1,0:T(1,128)} %bitcast.3) | data formatting | bytes 960
